TPU v7x, 32 devices: a whole 2x2x4 slice. The times are simulated.
32 devices in a mesh: cand: 4 (over y, core), hid: 8 (over z, x).
Axes of the slice: x: 2, y: 2, z: 4, core: 2. Of those that a mesh axis runs over, the one named last changes fastest.
Arguments:
- tokens: bfloat16 [4, 256, 2048], P('cand', None, 'hid'), may hold values from -6 to 6
- cotangent: bfloat16 [4, 256, 2048], P('cand', None, 'hid'), may hold values from -6 to 6
- gate_weight: bfloat16 [2048, 8192], P('cand', 'hid'), may hold values from -0.125 to 0.125
- up_weight: bfloat16 [2048, 8192], P('cand', 'hid'), may hold values from -0.125 to 0.125
- down_weight: bfloat16 [8192, 2048], P('hid', 'cand'), may hold values from -0.125 to 0.125
- width_steps: int32 [4], P('cand'), may hold values from 1 to 8
- block_order: int32 [8], replicated, may hold values from 0 to 7, each once
Outputs:
- grad_tokens: float32 [4, 256, 2048], P('cand', None, 'hid')
- grad_gate: float32 [2048, 8192], P('cand', 'hid')
- grad_up: float32 [2048, 8192], P('cand', 'hid')
- grad_down: float32 [8192, 2048], P('hid', 'cand')
Inputs may be any that keep to these rules, and one draw needn't show every extreme that they name: Candidate c uses the first width_steps[c] * 1024 logical hidden units. `block_order`: names each of the 8 logical blocks once.
All inputs are finite; a program needn't handle non-finite values.
Results may differ from a plain program's by a relative error of at most 0.02.
Values may be sent and summed in bfloat16 or wider, within the bound.
A program may use at most 64 MiB of HBM per device.

v0:
```python
import jax
import jax.numpy as jnp
from jax import lax
from jax.sharding import PartitionSpec as P

FF = 8192


def shards(tokens, cotangent, gate_weight, up_weight, down_weight, width_steps, block_order):
    inputs, upstream = (
        lax.all_gather(tokens, "hid", axis=2, tiled=True),
        lax.all_gather(cotangent, "hid", axis=2, tiled=True),
    )
    inputs = inputs[0]
    upstream = upstream[0]
    gate_full, up_full = (
        lax.all_gather(gate_weight, "cand", axis=0, tiled=True),
        lax.all_gather(up_weight, "cand", axis=0, tiled=True),
    )
    down_full = lax.all_gather(down_weight, "cand", axis=1, tiled=True)
    width = gate_weight.shape[1]
    places = jnp.arange(block_order.shape[0], dtype=jnp.int32)
    logical = jnp.sum(jnp.where(places == lax.axis_index("hid"), block_order, 0))
    active = logical * width < width_steps[0] * (FF // 8)
    keep = active.astype(jnp.float32)
    gate = jnp.dot(inputs, gate_full, preferred_element_type=jnp.float32)
    up = jnp.dot(inputs, up_full, preferred_element_type=jnp.float32)
    sig = jax.nn.sigmoid(gate)
    act = keep * gate * sig
    hidden = (act * up).astype(jnp.bfloat16)
    dhid = keep * jnp.einsum("td,fd->tf", upstream, down_full, preferred_element_type=jnp.float32)
    forward_d_up = (dhid * act).astype(jnp.bfloat16)
    forward_d_gate = (dhid * up * keep * sig * (1.0 + gate * (1.0 - sig))).astype(jnp.bfloat16)
    down_local = jnp.einsum("tf,td->fd", hidden, upstream, preferred_element_type=jnp.float32)
    down_local, d_gate, d_up = (down_local, forward_d_gate, forward_d_up)
    gate_local = jnp.einsum("td,tf->df", inputs, d_gate, preferred_element_type=jnp.float32)
    up_local = jnp.einsum("td,tf->df", inputs, d_up, preferred_element_type=jnp.float32)
    input_part = jnp.einsum("tf,df->td", d_gate, gate_full, preferred_element_type=jnp.float32)
    input_part = input_part + jnp.einsum(
        "tf,df->td", d_up, up_full, preferred_element_type=jnp.float32
    )
    gate_local, up_local, input_part = (gate_local, up_local, input_part)
    grad_tokens = lax.psum_scatter(
        input_part[None].astype(jnp.bfloat16), "hid", scatter_dimension=2, tiled=True
    ).astype(jnp.float32)
    grad_gate, grad_up = (
        lax.psum_scatter(
            gate_local.astype(jnp.bfloat16), "cand", scatter_dimension=0, tiled=True
        ).astype(jnp.float32),
        lax.psum_scatter(
            up_local.astype(jnp.bfloat16), "cand", scatter_dimension=0, tiled=True
        ).astype(jnp.float32),
    )
    grad_down = lax.psum_scatter(
        down_local.astype(jnp.bfloat16), "cand", scatter_dimension=1, tiled=True
    ).astype(jnp.float32)
    return (grad_tokens, grad_gate, grad_up, grad_down)


def solution(mesh):
    in_specs = (
        P("cand", None, "hid"),
        P("cand", None, "hid"),
        P("cand", "hid"),
        P("cand", "hid"),
        P("hid", "cand"),
        P("cand"),
        P(),
    )
    out_specs = (P("cand", None, "hid"), P("cand", "hid"), P("cand", "hid"), P("hid", "cand"))
    return jax.shard_map(shards, mesh=mesh, in_specs=in_specs, out_specs=out_specs, check_vma=False)
```

profile of v0, /device:TPU:0, one launch (start us, length us, event | category | flops | bytes accessed | tf_op | source)
XLA Modules:
  0.0 422.3 jit_solution(7583610765798703201)
XLA Ops:
  7.2 0.0 all-gather.10.cloned.1.call-start
  7.2 0.7 all-gather.10.cloned.1.call-update
  7.9 0.0 all-gather.12.cloned.1.call-start
  7.9 0.7 all-gather.12.cloned.1.call-update
  8.6 0.0 all-gather.14.cloned.1.call-start
  8.7 0.7 all-gather.14.cloned.1.call-update
  9.4 0.0 all-gather.6.cloned.1.call-start
  9.4 0.5 all-gather.6.cloned.1.call-update
  10.0 0.0 all-gather.8.cloned.1.call-start
  10.0 0.5 all-gather.8.cloned.1.call-update
  10.5 0.0 reduce-scatter.5.cloned.1.call-start
  11.2 1.3 fusion.10
  13.2 39.0 %all-gather.10.cloned.1.call-done = bf16[1,256,2048]{2,1,0:T(8,128)(2,1)} async-done(((bf16[1,256,256]{2,1,0:T(8,128)(2,1)}), bf16[1,256,2048]{2,1,0:T(8,128)(2,1)}) %all-gather.10.cloned.1.call-update) | async-done | bytes 1048592 | tf_op jit(solution)/shard_map/all_gather | solution.py:11
  52.2 0.0 copy-start
  52.2 35.1 %all-gather.12.cloned.1.call-done = bf16[2048,1024]{1,0:T(8,128)(2,1)} async-done(((bf16[512,1024]{1,0:T(8,128)(2,1)}), bf16[2048,1024]{1,0:T(8,128)(2,1)}) %all-gather.12.cloned.1.call-update) | async-done | bytes 4194320 | tf_op jit(solution)/shard_map/all_gather | solution.py:18
  87.2 3.8 fusion.6
  91.0 0.0 copy-start.4
  91.0 32.3 %all-gather.14.cloned.1.call-done = bf16[2048,1024]{1,0:T(8,128)(2,1)} async-done(((bf16[512,1024]{1,0:T(8,128)(2,1)}), bf16[2048,1024]{1,0:T(8,128)(2,1)}) %all-gather.14.cloned.1.call-update) | async-done | bytes 4194320 | tf_op jit(solution)/shard_map/all_gather | solution.py:17
  123.3 0.0 copy-done
  123.3 4.4 %fusion.4 = f32[256,1024]{1,0:T(8,128)} fusion(bf16[2048,1024]{1,0:T(8,128)(2,1)} %all-gather.14.cloned.1.call-done, bf16[1,256,2048]{2,1,0:T(8,128)(2,1)S(1)} %copy-done), kind=kOutput, calls=%fused_computation.9 | convolution fusion | flops 1073741824 | bytes 6291456 | tf_op jit(solution)/shard_map/dot_general | solution.py:26
  127.7 36.9 %all-gather.6.cloned.1.call-done = bf16[1,256,2048]{2,1,0:T(8,128)(2,1)} async-done(((bf16[1,256,256]{2,1,0:T(8,128)(2,1)}), bf16[1,256,2048]{2,1,0:T(8,128)(2,1)}) %all-gather.6.cloned.1.call-update) | async-done | bytes 1048592 | tf_op jit(solution)/shard_map/all_gather | solution.py:12
  164.6 34.9 %all-gather.8.cloned.1.call-done = bf16[1024,2048]{1,0:T(8,128)(2,1)} async-done(((bf16[1024,512]{1,0:T(8,128)(2,1)}), bf16[1024,2048]{1,0:T(8,128)(2,1)}) %all-gather.8.cloned.1.call-update) | async-done | bytes 4194320 | tf_op jit(solution)/shard_map/all_gather | solution.py:20
  199.5 0.0 copy-start.2
  199.5 4.6 %multiply_convert_fusion.1 = (bf16[256,1024]{1,0:T(8,128)(2,1)S(1)}, bf16[256,1024]{1,0:T(8,128)(2,1)S(1)}) fusion(f32[256,1024]{1,0:T(8,128)} %fusion.4, f32[]{:T(128)S(6)} %convert_element_type.45, f32[256,1024]{1,0:T(8,128)S(1)} %fusion.6, bf16[1024,2048]{1,0:T(8,128)(2,1)} %all-gather.8.cloned.1.call-done, ...), kind=kOutput, calls=%fused_computation.16 | convolution fusion | flops 1077936128 | bytes 8388612 | tf_op jit(solution)/shard_map/td,fd->tf/dot_general | solution.py:31
  204.1 0.0 copy-done.4
  204.1 0.0 copy-start.1
  204.1 0.0 copy-done.2
  204.2 1.3 fusion.12
  205.4 0.9 copy-done.1
  206.3 0.0 copy-start.3
  206.3 2.3 fusion.1
  208.6 0.0 reduce-scatter.5.cloned.1.call-update
  208.6 0.0 reduce-scatter.11.cloned.1.call-start
  208.7 0.0 copy-done.3
  208.7 4.9 %convolution_convert_fusion = bf16[1024,2048]{1,0:T(8,128)(2,1)} fusion(bf16[1,256,2048]{2,1,0:T(8,128)(2,1)S(1)} %copy-done.3, f32[256,1024]{1,0:T(8,128)} %copy-done.4, f32[256,1024]{1,0:T(8,128)} %fusion.4, f32[]{:T(128)S(6)} %convert_element_type.45), kind=kOutput, calls=%fused_computation.2 | convolution fusion | flops 1077673984 | bytes 7340036 | tf_op jit(solution)/shard_map/tf,td->fd/dot_general | solution.py:34
  213.5 0.0 reduce-scatter.11.cloned.1.call-update
  213.6 0.0 reduce-scatter.9.cloned.1.call-start
  213.6 3.3 convert_bitcast_fusion
  216.9 0.0 reduce-scatter.9.cloned.1.call-update
  216.9 0.0 reduce-scatter.7.cloned.1.call-start
  217.0 3.3 convert_bitcast_fusion.1
  220.2 0.0 reduce-scatter.7.cloned.1.call-update
  220.2 53.1 %reduce-scatter.5.cloned.1.call-done = bf16[1,256,256]{2,1,0:T(8,128)(2,1)} async-done(((bf16[1,256,2048]{2,1,0:T(8,128)(2,1)}), bf16[1,256,256]{2,1,0:T(8,128)(2,1)}) %reduce-scatter.5.cloned.1.call-update) | async-done | bytes 131088 | tf_op jit(solution)/shard_map/reduce_scatter | solution.py:43
  273.3 1.6 convert_element_type.50
  275.0 44.3 %reduce-scatter.11.cloned.1.call-done = bf16[1024,512]{1,0:T(8,128)(2,1)} async-done(((bf16[1024,2048]{1,0:T(8,128)(2,1)}), bf16[1024,512]{1,0:T(8,128)(2,1)}) %reduce-scatter.11.cloned.1.call-update) | async-done | bytes 1048592 | tf_op jit(solution)/shard_map/reduce_scatter | solution.py:54
  319.2 2.8 convert_element_type.59
  322.1 44.1 %reduce-scatter.9.cloned.1.call-done = bf16[512,1024]{0,1:T(8,128)(2,1)} async-done(((bf16[2048,1024]{0,1:T(8,128)(2,1)}), bf16[512,1024]{0,1:T(8,128)(2,1)}) %reduce-scatter.9.cloned.1.call-update) | async-done | bytes 1048592 | tf_op jit(solution)/shard_map/reduce_scatter | solution.py:50
  366.2 2.6 copy.12
  368.8 44.4 %reduce-scatter.7.cloned.1.call-done = bf16[512,1024]{0,1:T(8,128)(2,1)} async-done(((bf16[2048,1024]{0,1:T(8,128)(2,1)}), bf16[512,1024]{0,1:T(8,128)(2,1)}) %reduce-scatter.7.cloned.1.call-update) | async-done | bytes 1048592 | tf_op jit(solution)/shard_map/reduce_scatter | solution.py:47
  413.2 2.6 copy.11
Async XLA Ops:
  7.2 45.0 %all-gather.10.cloned.1.call-start = ((), (), s32[]{:S(2)}) async-start(), calls=%async_computation.6 | async-start | bytes 1179648 | tf_op jit(solution)/shard_map/all_gather | solution.py:11
  7.9 79.3 %all-gather.12.cloned.1.call-start = ((), (), s32[]{:S(2)}) async-start(), calls=%async_computation.7 | async-start | bytes 5242880 | tf_op jit(solution)/shard_map/all_gather | solution.py:18
  8.6 114.6 %all-gather.14.cloned.1.call-start = ((), (), s32[]{:S(2)}) async-start(), calls=%async_computation.8 | async-start | bytes 5242880 | tf_op jit(solution)/shard_map/all_gather | solution.py:17
  9.4 155.2 %all-gather.6.cloned.1.call-start = ((), (), s32[]{:S(2)}) async-start(), calls=%async_computation.4 | async-start | bytes 1179648 | tf_op jit(solution)/shard_map/all_gather | solution.py:12
  10.0 189.6 %all-gather.8.cloned.1.call-start = ((), (), s32[]{:S(2)}) async-start(), calls=%async_computation.5 | async-start | bytes 5242880 | tf_op jit(solution)/shard_map/all_gather | solution.py:20
  10.5 262.8 %reduce-scatter.5.cloned.1.call-start = ((), (), s32[]{:S(2)}) async-start(), calls=%async_computation.9 | async-start | bytes 1179648 | tf_op jit(solution)/shard_map/reduce_scatter | solution.py:43
  52.2 71.1 %copy-start = (bf16[1,256,2048]{2,1,0:T(8,128)(2,1)S(1)}, bf16[1,256,2048]{2,1,0:T(8,128)(2,1)}, u32[]{:S(2)}) copy-start(bf16[1,256,2048]{2,1,0:T(8,128)(2,1)} %all-gather.10.cloned.1.call-done) | copy-start | bytes 3145732
  91.0 113.1 %copy-start.4 = (f32[256,1024]{1,0:T(8,128)}, f32[256,1024]{1,0:T(8,128)S(1)}, u32[]{:S(2)}) copy-start(f32[256,1024]{1,0:T(8,128)S(1)} %fusion.6) | copy-start | bytes 3145732
  199.5 4.6 %copy-start.2 = (bf16[2048,1024]{1,0:T(8,128)(2,1)S(1)}, bf16[2048,1024]{1,0:T(8,128)(2,1)}, u32[]{:S(2)}) copy-start(bf16[2048,1024]{1,0:T(8,128)(2,1)} %all-gather.14.cloned.1.call-done) | copy-start | bytes 12582916
  204.1 2.2 copy-start.1
  206.3 2.3 copy-start.3
  208.6 110.6 %reduce-scatter.11.cloned.1.call-start = ((), (), s32[]{:S(2)}) async-start(), calls=%async_computation.12 | async-start | bytes 5242880 | tf_op jit(solution)/shard_map/reduce_scatter | solution.py:54
  213.6 152.6 %reduce-scatter.9.cloned.1.call-start = ((), (), s32[]{:S(2)}) async-start(), calls=%async_computation.11 | async-start | bytes 5242880 | tf_op jit(solution)/shard_map/reduce_scatter | solution.py:50
  216.9 196.3 %reduce-scatter.7.cloned.1.call-start = ((), (), s32[]{:S(2)}) async-start(), calls=%async_computation.10 | async-start | bytes 5242880 | tf_op jit(solution)/shard_map/reduce_scatter | solution.py:47
Sparse Core Ops, SparseCore 0:
  10.0 42.1 all-gather.9
  53.7 33.4 all-gather.11
  88.8 34.4 all-gather.13
  125.2 39.3 all-gather.5
  166.0 33.4 all-gather.7
  208.7 64.5 reduce-scatter.4
  275.9 43.3 reduce-scatter.10
  321.8 44.3 reduce-scatter.8
  368.7 44.3 reduce-scatter.6
where the time goes:
time: 423 us; the launch traced here: 422 us
  waiting for transfers between devices  367 us (87%)
  matrix products  27.7 us (7%)
  between operations  15.2 us (4%)
  local copies, waits for them, and re-layouts  6.02 us (1%)
  other arithmetic  5.75 us (1%)
    reduce_scatter x1, waiting for transfers between devices, shards(): lax.psum_scatter(input_part[None].astype(jnp.bfloat16), 'hid', scatter_di...  53.1 us
    reduce_scatter x1, waiting for transfers between devices, shards(): lax.psum_scatter(gate_local.astype(jnp.bfloat16), 'cand', scatter_dimensi...  44.4 us
    reduce_scatter x1, waiting for transfers between devices, shards(): lax.psum_scatter(down_local.astype(jnp.bfloat16), 'cand', scatter_dimensi...  44.3 us
    reduce_scatter x1, waiting for transfers between devices, shards(): lax.psum_scatter(up_local.astype(jnp.bfloat16), 'cand', scatter_dimension...  44.1 us
    all_gather x1, waiting for transfers between devices, shards(): lax.all_gather(tokens, 'hid', axis=2, tiled=True)  39 us
    all_gather x1, waiting for transfers between devices, shards(): lax.all_gather(cotangent, 'hid', axis=2, tiled=True)  36.9 us
    all_gather x1, waiting for transfers between devices, shards(): lax.all_gather(up_weight, 'cand', axis=0, tiled=True)  35.1 us
    all_gather x1, waiting for transfers between devices, shards(): down_full = lax.all_gather(down_weight, 'cand', axis=1, tiled=True)  34.9 us
  transfers between devices with their start and end apart: 9, of which 9 were waited for; matrix products, arithmetic and copies ran while one was open for 7% of the time, Pallas kernels for 0%

commit v1 on v0

--- a/solution.py
+++ b/solution.py
@@ -17,7 +17,12 @@
         lax.all_gather(gate_weight, "cand", axis=0, tiled=True),
         lax.all_gather(up_weight, "cand", axis=0, tiled=True),
     )
-    down_full = lax.all_gather(down_weight, "cand", axis=1, tiled=True)
+    ring = [down_weight]
+    for hop in range(3):
+        ring.append(lax.ppermute(ring[-1], "cand", [(dev, (dev + 1) % 4) for dev in range(4)]))
+    down_full = jnp.roll(
+        jnp.concatenate(ring[::-1], axis=1), (lax.axis_index("cand") + 1) * ring[0].shape[1], axis=1
+    )
     width = gate_weight.shape[1]
     places = jnp.arange(block_order.shape[0], dtype=jnp.int32)
     logical = jnp.sum(jnp.where(places == lax.axis_index("hid"), block_order, 0))

time: 423 us -> 387 us (0.915)
  waiting for transfers between devices: 367 us -> 318 us
  local copies, waits for them, and re-layouts: 6.02 us -> 18.7 us
    ppermute x0 -> x3, waiting for transfers between devices: none -> 40.4 us  [shards(): lax.ppermute(ring[-1], 'cand', [(dev, (dev + 1) % 4) for dev in range(4)])]
    all_gather x1, waiting for transfers between devices: 39 us -> 0.01 us  [shards(): lax.all_gather(tokens, 'hid', axis=2, tiled=True)]
    all_gather x1 -> x0, waiting for transfers between devices: 34.9 us -> none  [shards(): down_full = lax.all_gather(down_weight, 'cand', axis=1, tiled=True)]
    unnamed x12 -> x23, local copies, waits for them, and re-layouts: 6.02 us -> 17.5 us
    all_gather x1, waiting for transfers between devices: 32.3 us -> 22.5 us  [shards(): lax.all_gather(gate_weight, 'cand', axis=0, tiled=True)]
  transfers between devices with their start and end apart: 9 -> 11, of which waited for: 9 -> 10; matrix products, arithmetic and copies ran while one was open for 7% -> 10% of each run, Pallas kernels for 0% -> 0%
where the time goes in v1:
time: 387 us
  waiting for transfers between devices  318 us (82%)
  matrix products  28.2 us (7%)
  local copies, waits for them, and re-layouts  18.7 us (5%)
  between operations  15.6 us (4%)
  other arithmetic  5.75 us (1%)
    reduce_scatter x1, waiting for transfers between devices, shards(): lax.psum_scatter(input_part[None].astype(jnp.bfloat16), 'hid', scatter_di...  51.4 us
    reduce_scatter x1, waiting for transfers between devices, shards(): lax.psum_scatter(up_local.astype(jnp.bfloat16), 'cand', scatter_dimension...  44.4 us
    reduce_scatter x1, waiting for transfers between devices, shards(): lax.psum_scatter(down_local.astype(jnp.bfloat16), 'cand', scatter_dimensi...  44.4 us
    reduce_scatter x1, waiting for transfers between devices, shards(): lax.psum_scatter(gate_local.astype(jnp.bfloat16), 'cand', scatter_dimensi...  44.2 us
    ppermute x3, waiting for transfers between devices, shards(): lax.ppermute(ring[-1], 'cand', [(dev, (dev + 1) % 4) for dev in range(4)])  40.4 us
    all_gather x1, waiting for transfers between devices, shards(): lax.all_gather(cotangent, 'hid', axis=2, tiled=True)  36.4 us
    all_gather x1, waiting for transfers between devices, shards(): lax.all_gather(up_weight, 'cand', axis=0, tiled=True)  31.8 us
    all_gather x1, waiting for transfers between devices, shards(): lax.all_gather(gate_weight, 'cand', axis=0, tiled=True)  22.5 us
  transfers between devices with their start and end apart: 11, of which 10 were waited for; matrix products, arithmetic and copies ran while one was open for 10% of the time, Pallas kernels for 0%

profile of v1, /device:TPU:0, one launch (start us, length us, event | category | flops | bytes accessed | tf_op | source)
XLA Modules:
  0.0 386.9 jit_solution(14244680704641964696)
XLA Ops:
  7.2 0.0 all-gather.7.cloned.1.call-start
  7.2 0.7 all-gather.7.cloned.1.call-update
  7.9 0.0 copy-start
  7.9 0.0 all-gather.11.cloned.1.call-start
  8.0 0.7 all-gather.11.cloned.1.call-update
  8.7 0.0 all-gather.9.cloned.1.call-start
  8.7 0.7 all-gather.9.cloned.1.call-update
  9.4 0.0 all-gather.5.cloned.1.call-start
  9.4 0.5 collective-permute-start
  10.0 14.6 %collective-permute-done = bf16[1024,512]{1,0:T(8,128)(2,1)S(1)} collective-permute-done((bf16[1024,512]{1,0:T(8,128)(2,1)}, bf16[1024,512]{1,0:T(8,128)(2,1)S(1)}, u32[]{:S(2)}, u32[]{:S(2)}) %collective-permute-start) | collective-permute-done | bytes 1048608 | tf_op jit(solution)/shard_map/ppermute | solution.py:22
  24.6 0.0 collective-permute-start.1
  24.7 14.2 %collective-permute-done.1 = bf16[1024,512]{1,0:T(8,128)(2,1)S(1)} collective-permute-done((bf16[1024,512]{1,0:T(8,128)(2,1)S(1)}, bf16[1024,512]{1,0:T(8,128)(2,1)S(1)}, u32[]{:S(2)}, u32[]{:S(2)}) %collective-permute-start.1) | collective-permute-done | bytes 1048608 | tf_op jit(solution)/shard_map/ppermute | solution.py:22
  38.8 0.0 collective-permute-start.2
  38.8 0.0 all-gather.5.cloned.1.call-update
  38.9 0.0 reduce-scatter.5.cloned.1.call-start
  39.6 1.3 fusion.18
  41.5 11.6 %collective-permute-done.2 = bf16[1024,512]{1,0:T(8,128)(2,1)} collective-permute-done((bf16[1024,512]{1,0:T(8,128)(2,1)S(1)}, bf16[1024,512]{1,0:T(8,128)(2,1)}, u32[]{:S(2)}, u32[]{:S(2)}) %collective-permute-start.2) | collective-permute-done | bytes 1048608 | tf_op jit(solution)/shard_map/ppermute | solution.py:22
  53.2 2.3 constant_dynamic-update-slice_fusion.7
  55.5 1.2 constant_dynamic-update-slice_fusion.6
  56.7 1.1 constant_dynamic-update-slice_fusion.5
  57.8 0.0 copy-done
  57.8 1.1 constant_dynamic-update-slice_fusion.4
  58.9 2.4 constant_dynamic-update-slice_fusion.3
  61.3 1.1 constant_dynamic-update-slice_fusion.2
  62.5 1.1 constant_dynamic-update-slice_fusion.1
  63.6 1.1 constant_dynamic-update-slice_fusion
  64.7 0.0 all-gather.7.cloned.1.call-done
  64.7 0.0 copy-start.1
  64.7 22.5 %all-gather.11.cloned.1.call-done = bf16[2048,1024]{1,0:T(8,128)(2,1)} async-done(((bf16[512,1024]{1,0:T(8,128)(2,1)}), bf16[2048,1024]{1,0:T(8,128)(2,1)}) %all-gather.11.cloned.1.call-update) | async-done | bytes 4194320 | tf_op jit(solution)/shard_map/all_gather | solution.py:17
  87.2 4.2 %fusion.12 = f32[256,1024]{0,1:T(8,128)S(1)} fusion(bf16[2048,1024]{1,0:T(8,128)(2,1)} %all-gather.11.cloned.1.call-done, bf16[1,256,2048]{2,1,0:T(8,128)(2,1)} %all-gather.7.cloned.1.call-done), kind=kOutput, calls=%fused_computation.12 | convolution fusion | flops 1073741824 | bytes 6291456 | tf_op jit(solution)/shard_map/dot_general | solution.py:31
  91.5 0.0 copy-start.5
  91.5 31.8 %all-gather.9.cloned.1.call-done = bf16[2048,1024]{1,0:T(8,128)(2,1)} async-done(((bf16[512,1024]{1,0:T(8,128)(2,1)}), bf16[2048,1024]{1,0:T(8,128)(2,1)}) %all-gather.9.cloned.1.call-update) | async-done | bytes 4194320 | tf_op jit(solution)/shard_map/all_gather | solution.py:18
  123.3 0.0 copy-done.1
  123.3 4.9 %fusion.14 = f32[256,1024]{0,1:T(8,128)} fusion(bf16[2048,1024]{1,0:T(8,128)(2,1)} %all-gather.9.cloned.1.call-done, bf16[1,256,2048]{2,1,0:T(8,128)(2,1)S(1)} %copy-done.1), kind=kOutput, calls=%fused_computation.14 | convolution fusion | flops 1073741824 | bytes 6291456 | tf_op jit(solution)/shard_map/dot_general | solution.py:32
  128.2 36.4 %all-gather.5.cloned.1.call-done = bf16[1,256,2048]{2,1,0:T(8,128)(2,1)} async-done(((bf16[1,256,256]{2,1,0:T(8,128)(2,1)}), bf16[1,256,2048]{2,1,0:T(8,128)(2,1)}) %all-gather.5.cloned.1.call-update) | async-done | bytes 1048592 | tf_op jit(solution)/shard_map/all_gather | solution.py:12
  164.6 0.0 copy-start.2
  164.6 4.5 %multiply_convert_fusion.1 = (bf16[256,1024]{0,1:T(8,128)(2,1)S(1)}, bf16[256,1024]{0,1:T(8,128)(2,1)S(1)}) fusion(f32[256,1024]{0,1:T(8,128)S(1)} %fusion.12, f32[]{:T(128)S(6)} %convert_element_type.45, f32[256,1024]{0,1:T(8,128)} %fusion.14, bf16[1,256,2048]{2,1,0:T(8,128)(2,1)} %all-gather.5.cloned.1.call-done, ...), kind=kOutput, calls=%fused_computation.19 | convolution fusion | flops 1077936128 | bytes 8390144 | tf_op jit(solution)/shard_map/td,fd->tf/dot_general | solution.py:36
  169.1 0.0 copy-done.5
  169.1 0.0 copy-start.3
  169.1 0.0 copy-done.2
  169.2 1.3 fusion.21
  170.5 0.8 copy-done.3
  171.3 2.3 fusion.3
  173.6 0.0 reduce-scatter.5.cloned.1.call-update
  173.7 0.0 reduce-scatter.7.cloned.1.call-start
  173.7 3.2 convert_bitcast_fusion.1
  176.9 0.0 reduce-scatter.7.cloned.1.call-update
  176.9 0.0 copy-start.4
  177.0 0.0 reduce-scatter.9.cloned.1.call-start
  177.0 3.2 convert_bitcast_fusion
  180.2 0.0 reduce-scatter.9.cloned.1.call-update
  180.3 0.0 reduce-scatter.11.cloned.1.call-start
  180.3 0.0 copy-done.4
  180.3 1.1 copy-done.6
  181.5 4.5 %convolution_convert_fusion = bf16[1024,2048]{1,0:T(8,128)(2,1)} fusion(bf16[1,256,2048]{2,1,0:T(8,128)(2,1)S(1)} %copy-done.4, f32[256,1024]{0,1:T(8,128)} %fusion.14, f32[256,1024]{0,1:T(8,128)S(1)} %copy-done.6, f32[]{:T(128)S(6)} %convert_element_type.45), kind=kOutput, calls=%fused_computation.4 | convolution fusion | flops 1077673984 | bytes 7340036 | tf_op jit(solution)/shard_map/tf,td->fd/dot_general | solution.py:39
  186.0 0.0 reduce-scatter.11.cloned.1.call-update
  186.0 51.4 %reduce-scatter.5.cloned.1.call-done = bf16[1,256,256]{2,1,0:T(8,128)(2,1)} async-done(((bf16[1,256,2048]{2,1,0:T(8,128)(2,1)}), bf16[1,256,256]{2,1,0:T(8,128)(2,1)}) %reduce-scatter.5.cloned.1.call-update) | async-done | bytes 131088 | tf_op jit(solution)/shard_map/reduce_scatter | solution.py:48
  237.4 1.6 convert_element_type.50
  239.0 44.2 %reduce-scatter.7.cloned.1.call-done = bf16[512,1024]{0,1:T(8,128)(2,1)} async-done(((bf16[2048,1024]{0,1:T(8,128)(2,1)}), bf16[512,1024]{0,1:T(8,128)(2,1)}) %reduce-scatter.7.cloned.1.call-update) | async-done | bytes 1048592 | tf_op jit(solution)/shard_map/reduce_scatter | solution.py:52
  283.3 2.6 copy.16
  285.8 44.4 %reduce-scatter.9.cloned.1.call-done = bf16[512,1024]{0,1:T(8,128)(2,1)} async-done(((bf16[2048,1024]{0,1:T(8,128)(2,1)}), bf16[512,1024]{0,1:T(8,128)(2,1)}) %reduce-scatter.9.cloned.1.call-update) | async-done | bytes 1048592 | tf_op jit(solution)/shard_map/reduce_scatter | solution.py:55
  330.2 2.6 copy.17
  332.8 44.4 %reduce-scatter.11.cloned.1.call-done = bf16[1024,512]{1,0:T(8,128)(2,1)} async-done(((bf16[1024,2048]{1,0:T(8,128)(2,1)}), bf16[1024,512]{1,0:T(8,128)(2,1)}) %reduce-scatter.11.cloned.1.call-update) | async-done | bytes 1048592 | tf_op jit(solution)/shard_map/reduce_scatter | solution.py:59
  377.2 2.8 convert_element_type.59
  (1 shorter events, 0.0 us)
Async XLA Ops:
  7.2 57.6 %all-gather.7.cloned.1.call-start = ((), (), s32[]{:S(2)}) async-start(), calls=%async_computation.5 | async-start | bytes 1179648 | tf_op jit(solution)/shard_map/all_gather | solution.py:11
  7.9 49.9 %copy-start = (bf16[1024,512]{1,0:T(8,128)(2,1)S(1)}, bf16[1024,512]{1,0:T(8,128)(2,1)}, u32[]{:S(2)}) copy-start(bf16[1024,512]{1,0:T(8,128)(2,1)} %param.11) | copy-start | bytes 3145732
  7.9 79.3 %all-gather.11.cloned.1.call-start = ((), (), s32[]{:S(2)}) async-start(), calls=%async_computation.7 | async-start | bytes 5242880 | tf_op jit(solution)/shard_map/all_gather | solution.py:17
  8.7 114.6 %all-gather.9.cloned.1.call-start = ((), (), s32[]{:S(2)}) async-start(), calls=%async_computation.6 | async-start | bytes 5242880 | tf_op jit(solution)/shard_map/all_gather | solution.py:18
  9.4 155.2 %all-gather.5.cloned.1.call-start = ((), (), s32[]{:S(2)}) async-start(), calls=%async_computation.4 | async-start | bytes 1179648 | tf_op jit(solution)/shard_map/all_gather | solution.py:12
  9.4 15.2 %collective-permute-start = (bf16[1024,512]{1,0:T(8,128)(2,1)}, bf16[1024,512]{1,0:T(8,128)(2,1)S(1)}, u32[]{:S(2)}, u32[]{:S(2)}) collective-permute-start(bf16[1024,512]{1,0:T(8,128)(2,1)} %param.11), channel_id=1, source_target_pairs={{0,8},{8,16},{16,24},{24,0},{1,9},{9,17},{17,25},{25,1},{2,10},{10... | collective-permute-start | bytes 3145736 | tf_op jit(solution)/shard_map/ppermute | solution.py:22
  24.6 14.2 %collective-permute-start.1 = (bf16[1024,512]{1,0:T(8,128)(2,1)S(1)}, bf16[1024,512]{1,0:T(8,128)(2,1)S(1)}, u32[]{:S(2)}, u32[]{:S(2)}) collective-permute-start(bf16[1024,512]{1,0:T(8,128)(2,1)S(1)} %collective-permute-done), channel_id=1, source_target_pairs={{0,8},{8,16},{16,24},{24,0},{1,9},{9,17},{17,25},{25,1},{2,10},{10... | collective-permute-start | bytes 3145736 | tf_op jit(solution)/shard_map/ppermute | solution.py:22
  38.8 14.3 %collective-permute-start.2 = (bf16[1024,512]{1,0:T(8,128)(2,1)S(1)}, bf16[1024,512]{1,0:T(8,128)(2,1)}, u32[]{:S(2)}, u32[]{:S(2)}) collective-permute-start(bf16[1024,512]{1,0:T(8,128)(2,1)S(1)} %collective-permute-done.1), channel_id=1, source_target_pairs={{0,8},{8,16},{16,24},{24,0},{1,9},{9,17},{17,25},{25,1},{2,10},{10... | collective-permute-start | bytes 3145736 | tf_op jit(solution)/shard_map/ppermute | solution.py:22
  38.9 198.5 %reduce-scatter.5.cloned.1.call-start = ((), (), s32[]{:S(2)}) async-start(), calls=%async_computation.8 | async-start | bytes 1179648 | tf_op jit(solution)/shard_map/reduce_scatter | solution.py:48
  64.7 58.6 %copy-start.1 = (bf16[1,256,2048]{2,1,0:T(8,128)(2,1)S(1)}, bf16[1,256,2048]{2,1,0:T(8,128)(2,1)}, u32[]{:S(2)}) copy-start(bf16[1,256,2048]{2,1,0:T(8,128)(2,1)} %all-gather.7.cloned.1.call-done) | copy-start | bytes 3145732
  91.5 77.6 %copy-start.5 = (f32[256,1024]{0,1:T(8,128)}, f32[256,1024]{0,1:T(8,128)S(1)}, u32[]{:S(2)}) copy-start(f32[256,1024]{0,1:T(8,128)S(1)} %fusion.12) | copy-start | bytes 3145732
  164.6 4.5 %copy-start.2 = (bf16[2048,1024]{1,0:T(8,128)(2,1)S(1)}, bf16[2048,1024]{1,0:T(8,128)(2,1)}, u32[]{:S(2)}) copy-start(bf16[2048,1024]{1,0:T(8,128)(2,1)} %all-gather.11.cloned.1.call-done) | copy-start | bytes 12582916
  169.1 2.2 copy-start.3
  173.7 109.6 %reduce-scatter.7.cloned.1.call-start = ((), (), s32[]{:S(2)}) async-start(), calls=%async_computation.9 | async-start | bytes 5242880 | tf_op jit(solution)/shard_map/reduce_scatter | solution.py:52
  176.9 3.4 copy-start.4
  177.0 153.3 %reduce-scatter.9.cloned.1.call-start = ((), (), s32[]{:S(2)}) async-start(), calls=%async_computation.10 | async-start | bytes 5242880 | tf_op jit(solution)/shard_map/reduce_scatter | solution.py:55
  180.2 1.2 copy-start.6
  180.3 196.9 %reduce-scatter.11.cloned.1.call-start = ((), (), s32[]{:S(2)}) async-start(), calls=%async_computation.11 | async-start | bytes 5242880 | tf_op jit(solution)/shard_map/reduce_scatter | solution.py:59
Sparse Core Ops, SparseCore 0:
  10.0 42.1 all-gather.6
  53.7 33.4 all-gather.10
  88.8 34.4 all-gather.8
  125.2 39.3 all-gather.4
  173.8 63.5 reduce-scatter.4
  239.8 43.4 reduce-scatter.6
  285.8 44.3 reduce-scatter.8
  332.8 44.3 reduce-scatter.10
